TPU v7x, 32 devices: a whole 2x2x4 slice. The times are simulated.
32 devices in a mesh: seq: 8 (over y, x, core), fsdp: 4 (over z).
Axes of the slice: x: 2, y: 2, z: 4, core: 2. Of those that a mesh axis runs over, the one named last changes fastest.
Arguments:
- tokens: bfloat16 [4096, 1024], P(('seq', 'fsdp')), may hold values from -6 to 6
- first_gain: float32 [1024], P(('seq', 'fsdp')), may hold values from 0.5 to 1.5
- first_bias: float32 [1024], P(('seq', 'fsdp')), may hold values from -0.5 to 0.5
- w_qkv: float32 [1024, 3072], P(('seq', 'fsdp')), may hold values from -0.1875 to 0.1875
- query_bias: float32 [1024], P(('seq', 'fsdp')), may hold values from -0.5 to 0.5
- value_bias: float32 [1024], P(('seq', 'fsdp')), may hold values from -0.5 to 0.5
- w_proj: float32 [1024, 1024], P(('seq', 'fsdp')), may hold values from -0.75 to 0.75
- proj_bias: float32 [1024], P(('seq', 'fsdp')), may hold values from -0.5 to 0.5
- second_gain: float32 [1024], P(('seq', 'fsdp')), may hold values from 0.5 to 1.5
- second_bias: float32 [1024], P(('seq', 'fsdp')), may hold values from -0.5 to 0.5
- w_up: float32 [1024, 4096], P(('seq', 'fsdp')), may hold values from -0.1875 to 0.1875
- up_bias: float32 [4096], P(('seq', 'fsdp')), may hold values from -0.5 to 0.5
- w_down: float32 [4096, 1024], P(('seq', 'fsdp')), may hold values from -0.09375 to 0.09375
- down_bias: float32 [1024], P(('seq', 'fsdp')), may hold values from -0.5 to 0.5
- cotangent: bfloat16 [4096, 1024], P(('seq', 'fsdp')), may hold values from -6 to 6
- seq_ids: int32 [4096], P(('seq', 'fsdp')), may hold values from 0 to 31, as said below
- offsets: int32 [4096], P(('seq', 'fsdp')), may hold values from 0 to 511, as said below
Outputs:
- output: bfloat16 [4096, 1024], P(('seq', 'fsdp'))
- grad_tokens: bfloat16 [4096, 1024], P(('seq', 'fsdp'))
- grad_first_gain: float32 [1024], P(('seq', 'fsdp'))
- grad_first_bias: float32 [1024], P(('seq', 'fsdp'))
- grad_w_qkv: float32 [1024, 3072], P(('seq', 'fsdp'))
- grad_query_bias: float32 [1024], P(('seq', 'fsdp'))
- grad_value_bias: float32 [1024], P(('seq', 'fsdp'))
- grad_w_proj: float32 [1024, 1024], P(('seq', 'fsdp'))
- grad_proj_bias: float32 [1024], P(('seq', 'fsdp'))
- grad_second_gain: float32 [1024], P(('seq', 'fsdp'))
- grad_second_bias: float32 [1024], P(('seq', 'fsdp'))
- grad_w_up: float32 [1024, 4096], P(('seq', 'fsdp'))
- grad_up_bias: float32 [4096], P(('seq', 'fsdp'))
- grad_w_down: float32 [4096, 1024], P(('seq', 'fsdp'))
- grad_down_bias: float32 [1024], P(('seq', 'fsdp'))
Inputs may be any that keep to these rules, and one draw needn't show every extreme that they name: `seq_ids`: rows come in aligned blocks of 512 rows, each held by one group of fsdp devices; no sequence crosses a block. Half of the blocks, rounded up, hold one sequence of 512 rows; the others hold four sequences of 128 rows. Equal ids mark one sequence. `offsets`: the place of each row in its sequence, counting from 0.
All inputs are finite; a program needn't handle non-finite values.
Results may differ from a plain program's by a relative error of at most 0.012.
Values may be sent and summed in bfloat16 or wider, within the bound.
No kernel may reach another device: no remote copies, remote signals or barrier semaphores. Data moves between devices by JAX's collectives and lax.ppermute only.
A program may use at most 128 MiB of HBM per device.

v0:
```python
import math
import jax
import jax.numpy as jnp
from jax import lax
from jax.sharding import PartitionSpec as P

HEADS = 16
HDIM = 64
EPSILON = 1e-05


def layer_norm(values, gain, bias):
    centred = values - jnp.mean(values, axis=-1, keepdims=True)
    spread = jnp.mean(centred * centred, axis=-1, keepdims=True)
    return centred * lax.rsqrt(spread + EPSILON) * gain + bias


def gelu_tanh(values):
    return jax.nn.gelu(values, approximate=True)


def rows_dot(left, right):
    return lax.dot_general(
        left, right, (((0,), (0,)), ((), ())), preferred_element_type=jnp.float32
    )


def dot_back(left, right):
    return lax.dot_general(
        left, right, (((1,), (1,)), ((), ())), preferred_element_type=jnp.float32
    )


def gather_weights(w_qkv, w_proj, w_up, w_down):
    attn_pair = (
        lax.all_gather(w_qkv.astype(jnp.bfloat16), ("seq", "fsdp"), axis=0, tiled=True),
        lax.all_gather(w_proj.astype(jnp.bfloat16), ("seq", "fsdp"), axis=0, tiled=True),
    )
    mlp_pair = (
        lax.all_gather(w_up.astype(jnp.bfloat16), ("seq", "fsdp"), axis=0, tiled=True),
        lax.all_gather(w_down.astype(jnp.bfloat16), ("seq", "fsdp"), axis=0, tiled=True),
    )
    return (attn_pair[0], attn_pair[1], mlp_pair[0], mlp_pair[1])


def head_scores(queries, all_keys, visible):
    query_heads = queries.reshape(queries.shape[0], HEADS, HDIM)
    key_heads = all_keys.reshape(all_keys.shape[0], HEADS, HDIM)
    scores = jnp.einsum(
        "qhd,khd->hqk", query_heads, key_heads, preferred_element_type=jnp.float32
    ) * (1.0 / math.sqrt(HDIM))
    return jnp.where(visible[None], scores, jnp.float32(-1e30))


def forward_pass(tokens_f32, vectors, weights, seq_ids, offsets):
    (
        first_gain,
        first_bias,
        query_bias,
        value_bias,
        proj_bias,
        second_gain,
        second_bias,
        up_bias,
        down_bias,
    ) = vectors
    whole_qkv, whole_proj, whole_up, whole_down = weights
    model_width = tokens_f32.shape[1]
    normed = layer_norm(tokens_f32, first_gain, first_bias).astype(jnp.bfloat16)
    joined = jnp.dot(normed, whole_qkv, preferred_element_type=jnp.float32)
    queries = (joined[:, :model_width] + query_bias).astype(jnp.bfloat16)
    key_rows = joined[:, model_width : 2 * model_width].astype(jnp.bfloat16)
    value_rows = (joined[:, 2 * model_width :] + value_bias).astype(jnp.bfloat16)
    all_keys, all_values, key_ids, key_places = (
        lax.all_gather(key_rows, "fsdp", axis=0, tiled=True),
        lax.all_gather(value_rows, "fsdp", axis=0, tiled=True),
        lax.all_gather(seq_ids, "fsdp", axis=0, tiled=True),
        lax.all_gather(offsets, "fsdp", axis=0, tiled=True),
    )
    visible = (seq_ids[:, None] == key_ids[None, :]) & (key_places[None, :] <= offsets[:, None])
    scores = head_scores(queries, all_keys, visible)
    row_max = jnp.max(scores, axis=-1, keepdims=True)
    shifted = jnp.exp(scores - row_max)
    row_total = jnp.sum(shifted, axis=-1, keepdims=True)
    softmax_w = (shifted / row_total).astype(jnp.bfloat16)
    log_total = row_max + jnp.log(row_total)
    value_heads = all_values.reshape(all_values.shape[0], HEADS, HDIM)
    mixed_heads = jnp.einsum(
        "hqk,khd->qhd", softmax_w, value_heads, preferred_element_type=jnp.float32
    )
    mixed_heads = mixed_heads.reshape(queries.shape[0], model_width).astype(jnp.bfloat16)
    middle = (
        tokens_f32
        + jnp.dot(mixed_heads, whole_proj, preferred_element_type=jnp.float32)
        + proj_bias
    )
    second_normed = layer_norm(middle, second_gain, second_bias).astype(jnp.bfloat16)
    preact = jnp.dot(second_normed, whole_up, preferred_element_type=jnp.float32) + up_bias
    activated = gelu_tanh(preact).astype(jnp.bfloat16)
    result = middle + jnp.dot(activated, whole_down, preferred_element_type=jnp.float32) + down_bias
    return (
        result.astype(jnp.bfloat16),
        normed,
        queries,
        all_keys,
        all_values,
        visible,
        log_total,
        mixed_heads,
        middle,
        second_normed,
        preact,
        activated,
    )


def on_device(
    tokens,
    first_gain,
    first_bias,
    w_qkv,
    query_bias,
    value_bias,
    w_proj,
    proj_bias,
    second_gain,
    second_bias,
    w_up,
    up_bias,
    w_down,
    down_bias,
    cotangent,
    seq_ids,
    offsets,
):
    vectors = (
        lax.all_gather(first_gain, ("seq", "fsdp"), axis=0, tiled=True),
        lax.all_gather(first_bias, ("seq", "fsdp"), axis=0, tiled=True),
        lax.all_gather(query_bias, ("seq", "fsdp"), axis=0, tiled=True),
        lax.all_gather(value_bias, ("seq", "fsdp"), axis=0, tiled=True),
        lax.all_gather(proj_bias, ("seq", "fsdp"), axis=0, tiled=True),
        lax.all_gather(second_gain, ("seq", "fsdp"), axis=0, tiled=True),
        lax.all_gather(second_bias, ("seq", "fsdp"), axis=0, tiled=True),
        lax.all_gather(up_bias, ("seq", "fsdp"), axis=0, tiled=True),
        lax.all_gather(down_bias, ("seq", "fsdp"), axis=0, tiled=True),
    )
    tokens_f32 = tokens.astype(jnp.float32)
    weights = gather_weights(w_qkv, w_proj, w_up, w_down)
    stored = forward_pass(tokens_f32, vectors, weights, seq_ids, offsets)
    output = stored[0]
    weights = gather_weights(w_qkv, w_proj, w_up, w_down)
    stored = forward_pass(tokens_f32, vectors, weights, seq_ids, offsets)
    whole_qkv, whole_proj, whole_up, whole_down = weights
    (
        normed,
        queries,
        all_keys,
        all_values,
        visible,
        log_total,
        mixed_heads,
        middle,
        second_normed,
        preact,
        activated,
    ) = stored[1:]
    first_full, first_shift = (vectors[0], vectors[1])
    second_full, second_shift = (vectors[5], vectors[6])
    upstream = cotangent.astype(jnp.float32)
    row_count = tokens.shape[0]
    model_width = tokens.shape[1]
    grad_w_down = lax.psum_scatter(
        rows_dot(activated, cotangent), ("seq", "fsdp"), scatter_dimension=0, tiled=True
    )
    grad_act = dot_back(cotangent, whole_down)
    gelu_back = jax.vjp(gelu_tanh, preact)[1]
    grad_preact = gelu_back(grad_act)[0].astype(jnp.bfloat16)
    grad_w_up = lax.psum_scatter(
        rows_dot(second_normed, grad_preact), ("seq", "fsdp"), scatter_dimension=0, tiled=True
    )
    grad_second = dot_back(grad_preact, whole_up)
    second_back = jax.vjp(layer_norm, middle, second_full, second_shift)[1]
    grad_mid_norm, grad_second_gain, grad_second_bias = second_back(grad_second)
    grad_middle = upstream + grad_mid_norm
    grad_attended = grad_middle.astype(jnp.bfloat16)
    grad_w_proj = lax.psum_scatter(
        rows_dot(mixed_heads, grad_attended), ("seq", "fsdp"), scatter_dimension=0, tiled=True
    )
    grad_mixed = dot_back(grad_attended, whole_proj).astype(jnp.bfloat16)
    mixed_grad_heads = grad_mixed.reshape(row_count, HEADS, HDIM)
    value_heads = all_values.reshape(all_values.shape[0], HEADS, HDIM)
    key_heads = all_keys.reshape(all_keys.shape[0], HEADS, HDIM)
    query_heads = queries.reshape(row_count, HEADS, HDIM)
    scores = head_scores(queries, all_keys, visible)
    softmax_f = jnp.exp(scores - log_total)
    grad_probs = jnp.einsum(
        "qhd,khd->hqk", mixed_grad_heads, value_heads, preferred_element_type=jnp.float32
    )
    row_delta = jnp.sum(grad_probs * softmax_f, axis=-1, keepdims=True)
    grad_scores = (softmax_f * (grad_probs - row_delta)).astype(jnp.bfloat16)
    score_scale = 1.0 / math.sqrt(HDIM)
    grad_queries = (
        jnp.einsum("hqk,khd->qhd", grad_scores, key_heads, preferred_element_type=jnp.float32)
        * score_scale
    )
    grad_queries = grad_queries.reshape(row_count, model_width).astype(jnp.bfloat16)
    key_part = (
        jnp.einsum("hqk,qhd->khd", grad_scores, query_heads, preferred_element_type=jnp.float32)
        * score_scale
    )
    value_part = jnp.einsum(
        "hqk,qhd->khd",
        softmax_f.astype(jnp.bfloat16),
        mixed_grad_heads,
        preferred_element_type=jnp.float32,
    )
    key_count = all_keys.shape[0]
    grad_keys, grad_values = (
        lax.psum_scatter(
            key_part.reshape(key_count, model_width).astype(jnp.bfloat16),
            "fsdp",
            scatter_dimension=0,
            tiled=True,
        ).astype(jnp.float32),
        lax.psum_scatter(
            value_part.reshape(key_count, model_width).astype(jnp.bfloat16),
            "fsdp",
            scatter_dimension=0,
            tiled=True,
        ).astype(jnp.float32),
    )
    grad_keys = grad_keys.astype(jnp.bfloat16)
    grad_values = grad_values.astype(jnp.bfloat16)
    grad_joined = jnp.concatenate([grad_queries, grad_keys, grad_values], axis=1)
    grad_w_qkv = lax.psum_scatter(
        rows_dot(normed, grad_joined), ("seq", "fsdp"), scatter_dimension=0, tiled=True
    )
    grad_first = dot_back(grad_joined, whole_qkv)
    first_back = jax.vjp(layer_norm, tokens_f32, first_full, first_shift)[1]
    grad_tok_norm, grad_first_gain, grad_first_bias = first_back(grad_first)
    grad_tokens = (grad_middle + grad_tok_norm).astype(jnp.bfloat16)
    vector_sums = (
        lax.psum_scatter(grad_first_gain, ("seq", "fsdp"), scatter_dimension=0, tiled=True),
        lax.psum_scatter(grad_first_bias, ("seq", "fsdp"), scatter_dimension=0, tiled=True),
        lax.psum_scatter(
            jnp.sum(grad_queries.astype(jnp.float32), axis=0),
            ("seq", "fsdp"),
            scatter_dimension=0,
            tiled=True,
        ),
        lax.psum_scatter(
            jnp.sum(grad_values.astype(jnp.float32), axis=0),
            ("seq", "fsdp"),
            scatter_dimension=0,
            tiled=True,
        ),
        lax.psum_scatter(
            jnp.sum(grad_attended.astype(jnp.float32), axis=0),
            ("seq", "fsdp"),
            scatter_dimension=0,
            tiled=True,
        ),
        lax.psum_scatter(grad_second_gain, ("seq", "fsdp"), scatter_dimension=0, tiled=True),
        lax.psum_scatter(grad_second_bias, ("seq", "fsdp"), scatter_dimension=0, tiled=True),
        lax.psum_scatter(
            jnp.sum(grad_preact.astype(jnp.float32), axis=0),
            ("seq", "fsdp"),
            scatter_dimension=0,
            tiled=True,
        ),
        lax.psum_scatter(
            jnp.sum(upstream, axis=0), ("seq", "fsdp"), scatter_dimension=0, tiled=True
        ),
    )
    return (
        output,
        grad_tokens,
        vector_sums[0],
        vector_sums[1],
        grad_w_qkv,
        vector_sums[2],
        vector_sums[3],
        grad_w_proj,
        vector_sums[4],
        vector_sums[5],
        vector_sums[6],
        grad_w_up,
        vector_sums[7],
        grad_w_down,
        vector_sums[8],
    )


def solution(mesh):
    placed = (
        P(("seq", "fsdp"), None),
        P(("seq", "fsdp")),
        P(("seq", "fsdp")),
        P(("seq", "fsdp"), None),
        P(("seq", "fsdp")),
        P(("seq", "fsdp")),
        P(("seq", "fsdp"), None),
        P(("seq", "fsdp")),
        P(("seq", "fsdp")),
        P(("seq", "fsdp")),
        P(("seq", "fsdp"), None),
        P(("seq", "fsdp")),
        P(("seq", "fsdp"), None),
        P(("seq", "fsdp")),
        P(("seq", "fsdp"), None),
        P(("seq", "fsdp")),
        P(("seq", "fsdp")),
    )
    return jax.shard_map(
        on_device,
        mesh=mesh,
        in_specs=placed,
        out_specs=(
            P(("seq", "fsdp"), None),
            P(("seq", "fsdp"), None),
            P(("seq", "fsdp")),
            P(("seq", "fsdp")),
            P(("seq", "fsdp"), None),
            P(("seq", "fsdp")),
            P(("seq", "fsdp")),
            P(("seq", "fsdp"), None),
            P(("seq", "fsdp")),
            P(("seq", "fsdp")),
            P(("seq", "fsdp")),
            P(("seq", "fsdp"), None),
            P(("seq", "fsdp")),
            P(("seq", "fsdp"), None),
            P(("seq", "fsdp")),
        ),
        check_vma=False,
    )
```

profile of v0, /device:TPU:0, one launch (start us, length us, event | category | flops | bytes accessed | tf_op | source)
XLA Modules:
  0.0 1482.5 jit_solution(7892040546038730555)
XLA Ops:
  14.9 42.7 %all-reduce.18 = (f32[1024]{0:T(1024)S(1)}, f32[1024]{0:T(1024)S(1)}, f32[1024]{0:T(1024)S(1)}, f32[1024]{0:T(1024)S(1)}, f32[1024]{0:T(1024)S(1)}, /*index=5*/f32[1024]{0:T(1024)S(1)}, f32[1024]{0:T(1024)S(1)}) all-reduce(f32[1024]{0:T(1024)S(1)} %dynamic-update-slice.1, ...), channel_id=1, replica_groups=mesh['seq'=8,'fsdp'=4] {'seq','fsdp'}, use_global_device_ids=true, to_apply=%add.1 | all-reduce | flops 7168 | bytes 57344
  59.8 23.8 %all-gather.10.cloned.1.call-done = bf16[1024,3072]{1,0:T(8,128)(2,1)} async-done(((bf16[32,3072]{1,0:T(8,128)(2,1)}), bf16[1024,3072]{1,0:T(8,128)(2,1)}) %all-gather.10.cloned.1.call-update) | async-done | bytes 6291472 | tf_op jit(solution)/shard_map/all_gather | solution.py:36
  83.7 4.0 fusion.42
  91.7 9.6 all-gather.1
  101.3 8.0 all-gather
  109.3 65.8 %all-gather.2 = f32[32,1,128]{2,1,0:T(1,128)S(1)} all-gather(f32[1,1,128]{2,1,0:T(1,128)S(1)} %bitcast.69), channel_id=1, replica_groups=mesh['seq'=8,'fsdp'=4] {'seq','fsdp'}, dimensions={0}, use_global_device_ids=true | all-gather | bytes 16896 | tf_op jit(solution)/shard_map/all_gather | solution.py:144
  183.2 20.8 %all-gather.16.cloned.1.call-done = bf16[1024,1024]{1,0:T(8,128)(2,1)} async-done(((bf16[32,1024]{1,0:T(8,128)(2,1)}), bf16[1024,1024]{1,0:T(8,128)(2,1)}) %all-gather.16.cloned.1.call-update) | async-done | bytes 2097168 | tf_op jit(solution)/shard_map/all_gather | solution.py:37
  206.4 76.9 %all-gather.20.cloned.1.call-done = bf16[4096,1024]{1,0:T(8,128)(2,1)} async-done(((bf16[128,1024]{1,0:T(8,128)(2,1)}), bf16[4096,1024]{1,0:T(8,128)(2,1)}) %all-gather.20.cloned.1.call-update) | async-done | bytes 8388624 | tf_op jit(solution)/shard_map/all_gather | solution.py:41
  283.3 7.5 fusion.53
  290.8 71.6 %all-gather.18.cloned.1.call-done = bf16[1024,4096]{1,0:T(8,128)(2,1)} async-done(((bf16[32,4096]{1,0:T(8,128)(2,1)}), bf16[1024,4096]{1,0:T(8,128)(2,1)}) %all-gather.18.cloned.1.call-update) | async-done | bytes 8388624 | tf_op jit(solution)/shard_map/all_gather | solution.py:40
  362.4 8.4 convert_reduce_fusion
  376.6 4.2 fusion.13
  398.6 10.5 reduce-scatter.21.cloned.1.call-done
  410.3 27.0 %reduce-scatter.19.cloned.1.call-done = bf16[128,1024]{1,0:T(8,128)(2,1)} async-done(((bf16[512,1024]{1,0:T(8,128)(2,1)}), bf16[128,1024]{1,0:T(8,128)(2,1)}) %reduce-scatter.19.cloned.1.call-update) | async-done | bytes 262160
  438.4 7.5 fusion.35
  446.8 9.7 fusion.46
  457.7 8.2 fusion.45
  467.0 5.1 fusion.47
  473.4 40.2 %all-reduce.17 = (f32[1024]{0:T(1024)S(1)}, f32[1024]{0:T(1024)S(1)}, f32[1024]{0:T(1024)S(1)}, f32[1024]{0:T(1024)S(1)}, f32[1024]{0:T(1024)S(1)}, /*index=5*/f...) all-reduce(f32[1024]{0:T(1024)S(1)} %dynamic-update-slice.7, ...), channel_id=1, replica_groups=mesh['seq'=8,'fsdp'=4] {'seq','fsdp'}, use_global_device_ids=true, to_apply=%add.7 | all-reduce | flops 13312 | bytes 106496
  518.8 6.3 fusion.18
  525.2 63.4 %reduce-scatter.13.cloned.1.call-done = f32[32,1024]{1,0:T(8,128)} async-done(((f32[1024,1024]{1,0:T(8,128)}), f32[32,1024]{1,0:T(8,128)}) %reduce-scatter.13.cloned.1.call-update) | async-done | bytes 131088 | tf_op jit(solution)/shard_map/reduce_scatter | solution.py:186
  588.6 159.9 %reduce-scatter.11.cloned.1.call-done = f32[32,3072]{1,0:T(8,128)} async-done(((f32[1024,3072]{1,0:T(8,128)}), f32[32,3072]{1,0:T(8,128)}) %reduce-scatter.11.cloned.1.call-update) | async-done | bytes 393232 | tf_op jit(solution)/shard_map/reduce_scatter | solution.py:235
  748.4 362.5 %reduce-scatter.17.cloned.1.call-done = f32[128,1024]{1,0:T(8,128)} async-done(((f32[4096,1024]{1,0:T(8,128)}), f32[128,1024]{1,0:T(8,128)}) %reduce-scatter.17.cloned.1.call-update) | async-done | bytes 524304 | tf_op jit(solution)/shard_map/reduce_scatter | solution.py:172
  1110.9 364.7 %reduce-scatter.15.cloned.1.call-done = f32[32,4096]{1,0:T(8,128)} async-done(((f32[1024,4096]{1,0:T(8,128)}), f32[32,4096]{1,0:T(8,128)}) %reduce-scatter.15.cloned.1.call-update) | async-done | bytes 524304 | tf_op jit(solution)/shard_map/reduce_scatter | solution.py:178
  (143 shorter events, 59.8 us)
Async XLA Ops:
  7.2 76.5 %all-gather.10.cloned.1.call-start = ((), (), s32[]{:S(2)}) async-start(), calls=%async_computation.6 | async-start | bytes 6488064 | tf_op jit(solution)/shard_map/all_gather | solution.py:36
  8.9 166.5 %all-gather.12.cloned.1.call-start = ((), (), s32[]{:S(2)}) async-start(), calls=%async_computation.7 | async-start | bytes 1310720 | tf_op jit(solution)/shard_map/all_gather | solution.py:76
  87.6 3.3 copy-start.18
  88.5 3.3 copy-start.20
  88.5 12.8 copy-start.21
  88.5 20.8 %copy-start.22 = (f32[128]{0:T(128)S(1)}, f32[128]{0:T(128)}, u32[]{:S(2)}) copy-start(f32[128]{0:T(128)} %param.28) | copy-start | bytes 1540
  88.5 88.6 %all-gather.14.cloned.1.call-start = ((), (), s32[]{:S(2)}) async-start(), calls=%async_computation.8 | async-start | bytes 1310720 | tf_op jit(solution)/shard_map/all_gather | solution.py:75
  89.3 114.7 %all-gather.16.cloned.1.call-start = ((), (), s32[]{:S(2)}) async-start(), calls=%async_computation.9 | async-start | bytes 2162688 | tf_op jit(solution)/shard_map/all_gather | solution.py:37
  90.0 193.3 %all-gather.20.cloned.1.call-start = ((), (), s32[]{:S(2)}) async-start(), calls=%async_computation.11 | async-start | bytes 8650752 | tf_op jit(solution)/shard_map/all_gather | solution.py:41
  90.9 271.5 %all-gather.18.cloned.1.call-start = ((), (), s32[]{:S(2)}) async-start(), calls=%async_computation.10 | async-start | bytes 8650752 | tf_op jit(solution)/shard_map/all_gather | solution.py:40
  91.7 317.5 %reduce-scatter.21.cloned.1.call-start = ((), (), s32[]{:S(2)}) async-start(), calls=%async_computation.17 | async-start | bytes 1310720
  175.4 3.2 copy-start.11
  181.5 22.5 %copy-start.2 = (bf16[128,1024]{1,0:T(8,128)(2,1)S(1)}, bf16[128,1024]{1,0:T(8,128)(2,1)}, u32[]{:S(2)}) copy-start(bf16[128,1024]{1,0:T(8,128)(2,1)} %param.17) | copy-start | bytes 786436
  183.2 107.7 %copy-start.15 = (bf16[16,64,128]{2,1,0:T(8,128)(2,1)}, bf16[16,64,128]{2,1,0:T(8,128)(2,1)S(1)}, u32[]{:S(2)}) copy-start(bf16[16,64,128]{2,1,0:T(8,128)(2,1)S(1)} %fusion.20) | copy-start | bytes 786436
  183.2 100.1 %copy-start.8 = (bf16[128,1024]{1,0:T(8,128)(2,1)S(1)}, bf16[128,1024]{1,0:T(8,128)(2,1)}, u32[]{:S(2)}) copy-start(bf16[128,1024]{1,0:T(8,128)(2,1)} %param.31) | copy-start | bytes 786436
  362.4 8.4 copy-start.5
  374.3 6.4 copy-start.10
  383.1 54.2 %reduce-scatter.19.cloned.1.call-start = ((), (), s32[]{:S(2)}) async-start(), calls=%async_computation.16 | async-start | bytes 1310720
  383.1 3.8 copy-start.1
  391.7 196.9 %reduce-scatter.13.cloned.1.call-start = ((), (), s32[]{:S(2)}) async-start(), calls=%async_computation.13 | async-start | bytes 4325376 | tf_op jit(solution)/shard_map/reduce_scatter | solution.py:186
  395.8 352.6 %reduce-scatter.11.cloned.1.call-start = ((), (), s32[]{:S(2)}) async-start(), calls=%async_computation.12 | async-start | bytes 12976128 | tf_op jit(solution)/shard_map/reduce_scatter | solution.py:235
  438.4 7.5 copy-start.13
  445.9 665.0 %reduce-scatter.17.cloned.1.call-start = ((), (), s32[]{:S(2)}) async-start(), calls=%async_computation.15 | async-start | bytes 17301504 | tf_op jit(solution)/shard_map/reduce_scatter | solution.py:172
  456.5 1019.1 %reduce-scatter.15.cloned.1.call-start = ((), (), s32[]{:S(2)}) async-start(), calls=%async_computation.14 | async-start | bytes 17301504 | tf_op jit(solution)/shard_map/reduce_scatter | solution.py:178
  (12 other events, 17.8 us)
Sparse Core Ops, SparseCore 0:
  11.4 72.1 all-gather.9
  88.6 26.5 all-gather.11
  117.4 27.4 all-gather.13
  148.2 55.7 all-gather.15
  207.3 75.9 all-gather.19
  286.7 75.6 all-gather.17
  383.2 25.9 reduce-scatter.20
  411.4 25.7 reduce-scatter.18
  440.1 148.4 reduce-scatter.12
  595.0 153.3 reduce-scatter.10
  751.3 359.5 reduce-scatter.16
  1113.6 361.9 reduce-scatter.14
where the time goes:
time: 1480 us
  waiting for transfers between devices  1180 us (80%)
  blocking collectives  166 us (11%)
  matrix products  81.2 us (5%)
  local copies, waits for them, and re-layouts  27 us (2%)
    reduce_scatter x1, waiting for transfers between devices, on_device(): lax.psum_scatter(rows_dot(second_normed, grad_preact), ('seq', 'fsdp'), s...  365 us
    reduce_scatter x1, waiting for transfers between devices, on_device(): lax.psum_scatter(rows_dot(activated, cotangent), ('seq', 'fsdp'), scatter...  362 us
    reduce_scatter x1, waiting for transfers between devices, on_device(): lax.psum_scatter(rows_dot(normed, grad_joined), ('seq', 'fsdp'), scatter_...  160 us
    unnamed x2, blocking collectives  82.9 us
    all_gather x1, waiting for transfers between devices, gather_weights(): lax.all_gather(w_down.astype(jnp.bfloat16), ('seq', 'fsdp'), axis=0, tile...  76.9 us
    all_gather x1, waiting for transfers between devices, gather_weights(): lax.all_gather(w_up.astype(jnp.bfloat16), ('seq', 'fsdp'), axis=0, tiled=...  71.6 us
    all_gather x1, blocking collectives, on_device(): lax.all_gather(up_bias, ('seq', 'fsdp'), axis=0, tiled=True)  65.8 us
    reduce_scatter x1, waiting for transfers between devices, on_device(): lax.psum_scatter(rows_dot(mixed_heads, grad_attended), ('seq', 'fsdp'), s...  63.4 us
  transfers between devices with their start and end apart: 12, of which 10 were waited for; matrix products, arithmetic and copies ran while one was open for 6% of the time, Pallas kernels for 0%

commit v1 on v0

--- a/solution.py
+++ b/solution.py
@@ -7,6 +7,18 @@
 HEADS = 16
 HDIM = 64
 EPSILON = 1e-05
+
+
+def gather_by_bits(x, axis, dim):
+    ways, here = (lax.axis_size(axis), lax.axis_index(axis))
+    grown, reach = (x, 1)
+    while reach < ways:
+        theirs = lax.ppermute(grown, axis, [(d, d ^ reach) for d in range(ways)])
+        mine_first = jnp.concatenate([grown, theirs], axis=dim)
+        theirs_first = jnp.concatenate([theirs, grown], axis=dim)
+        grown = jnp.where(here & reach == 0, mine_first, theirs_first)
+        reach = 2 * reach
+    return grown
 
 
 def layer_norm(values, gain, bias):
@@ -141,7 +153,7 @@
         lax.all_gather(proj_bias, ("seq", "fsdp"), axis=0, tiled=True),
         lax.all_gather(second_gain, ("seq", "fsdp"), axis=0, tiled=True),
         lax.all_gather(second_bias, ("seq", "fsdp"), axis=0, tiled=True),
-        lax.all_gather(up_bias, ("seq", "fsdp"), axis=0, tiled=True),
+        gather_by_bits(up_bias, ("seq", "fsdp"), 0),
         lax.all_gather(down_bias, ("seq", "fsdp"), axis=0, tiled=True),
     )
     tokens_f32 = tokens.astype(jnp.float32)

time: 1480 us -> 1480 us (level)
  blocking collectives: 166 us -> 101 us
  waiting for transfers between devices: 1180 us -> 1240 us
    all_gather x1 -> x0, blocking collectives: 65.8 us -> none  [on_device(): lax.all_gather(up_bias, ('seq', 'fsdp'), axis=0, tiled=True)]
    all_gather x1, waiting for transfers between devices: 20.8 us -> 53.2 us  [gather_weights(): lax.all_gather(w_proj.astype(jnp.bfloat16), ('seq', 'fsdp'), axis=0, tile...]
    all_gather x1, waiting for transfers between devices: 0.02 us -> 19.2 us  [forward_pass(): lax.all_gather(key_rows, 'fsdp', axis=0, tiled=True)]
  transfers between devices with their start and end apart: 12 -> 17, of which waited for: 10 -> 15; matrix products, arithmetic and copies ran while one was open for 6% -> 6% of each run, Pallas kernels for 0% -> 0%
where the time goes in v1:
time: 1480 us
  waiting for transfers between devices  1240 us (84%)
  blocking collectives  101 us (7%)
  matrix products  76.4 us (5%)
  local copies, waits for them, and re-layouts  26.6 us (2%)
    reduce_scatter x1, waiting for transfers between devices, on_device(): lax.psum_scatter(rows_dot(second_normed, grad_preact), ('seq', 'fsdp'), s...  365 us
    reduce_scatter x1, waiting for transfers between devices, on_device(): lax.psum_scatter(rows_dot(activated, cotangent), ('seq', 'fsdp'), scatter...  362 us
    reduce_scatter x1, waiting for transfers between devices, on_device(): lax.psum_scatter(rows_dot(normed, grad_joined), ('seq', 'fsdp'), scatter_...  160 us
    unnamed x2, blocking collectives  83.1 us
    all_gather x1, waiting for transfers between devices, gather_weights(): lax.all_gather(w_up.astype(jnp.bfloat16), ('seq', 'fsdp'), axis=0, tiled=...  76.9 us
    all_gather x1, waiting for transfers between devices, gather_weights(): lax.all_gather(w_down.astype(jnp.bfloat16), ('seq', 'fsdp'), axis=0, tile...  74.3 us
    reduce_scatter x1, waiting for transfers between devices, on_device(): lax.psum_scatter(rows_dot(mixed_heads, grad_attended), ('seq', 'fsdp'), s...  62.1 us
    all_gather x1, waiting for transfers between devices, gather_weights(): lax.all_gather(w_proj.astype(jnp.bfloat16), ('seq', 'fsdp'), axis=0, tile...  53.2 us
  transfers between devices with their start and end apart: 17, of which 15 were waited for; matrix products, arithmetic and copies ran while one was open for 6% of the time, Pallas kernels for 0%

profile of v1, /device:TPU:0, one launch (start us, length us, event | category | flops | bytes accessed | tf_op | source)
XLA Modules:
  0.0 1479.7 jit_solution(5995670709961864967)
XLA Ops:
  14.9 42.7 %all-reduce.18 = (f32[1024]{0:T(1024)S(1)}, f32[1024]{0:T(1024)S(1)}, f32[1024]{0:T(1024)S(1)}, f32[1024]{0:T(1024)S(1)}, f32[1024]{0:T(1024)S(1)}, /*index=5*/f32[1024]{0:T(1024)S(1)}, f32[1024]{0:T(1024)S(1)}) all-reduce(f32[1024]{0:T(1024)S(1)} %dynamic-update-slice.1, ...), channel_id=1, replica_groups=mesh['seq'=8,'fsdp'=4] {'seq','fsdp'}, use_global_device_ids=true, to_apply=%add.1 | all-reduce | flops 7168 | bytes 57344
  59.8 23.8 %all-gather.9.cloned.1.call-done = bf16[1024,3072]{1,0:T(8,128)(2,1)} async-done(((bf16[32,3072]{1,0:T(8,128)(2,1)}), bf16[1024,3072]{1,0:T(8,128)(2,1)}) %all-gather.9.cloned.1.call-update) | async-done | bytes 6291472 | tf_op jit(solution)/shard_map/all_gather | solution.py:48
  83.7 4.0 fusion.42
  102.5 9.9 all-gather.1
  112.4 7.6 all-gather
  125.6 19.2 %all-gather.13.cloned.1.call-done = bf16[512,1024]{1,0:T(8,128)(2,1)} async-done(((bf16[128,1024]{1,0:T(8,128)(2,1)}), bf16[512,1024]{1,0:T(8,128)(2,1)}) %all-gather.13.cloned.1.call-update) | async-done | bytes 1048592 | tf_op jit(solution)/shard_map/all_gather | solution.py:87
  150.8 53.2 %all-gather.15.cloned.1.call-done = bf16[1024,1024]{1,0:T(8,128)(2,1)} async-done(((bf16[32,1024]{1,0:T(8,128)(2,1)}), bf16[1024,1024]{1,0:T(8,128)(2,1)}) %all-gather.15.cloned.1.call-update) | async-done | bytes 2097168 | tf_op jit(solution)/shard_map/all_gather | solution.py:49
  206.3 76.9 %all-gather.17.cloned.1.call-done = bf16[1024,4096]{1,0:T(8,128)(2,1)} async-done(((bf16[32,4096]{1,0:T(8,128)(2,1)}), bf16[1024,4096]{1,0:T(8,128)(2,1)}) %all-gather.17.cloned.1.call-update) | async-done | bytes 8388624 | tf_op jit(solution)/shard_map/all_gather | solution.py:52
  283.2 4.8 fusion.46
  288.0 74.3 %all-gather.19.cloned.1.call-done = bf16[4096,1024]{1,0:T(8,128)(2,1)} async-done(((bf16[128,1024]{1,0:T(8,128)(2,1)}), bf16[4096,1024]{1,0:T(8,128)(2,1)}) %all-gather.19.cloned.1.call-update) | async-done | bytes 8388624 | tf_op jit(solution)/shard_map/all_gather | solution.py:53
  362.3 7.2 convert_reduce_fusion
  380.8 3.9 multiply_reduce_fusion
  396.2 10.7 reduce-scatter.21.cloned.1.call-done
  408.0 27.0 %reduce-scatter.19.cloned.1.call-done = bf16[128,1024]{1,0:T(8,128)(2,1)} async-done(((bf16[512,1024]{1,0:T(8,128)(2,1)}), bf16[128,1024]{1,0:T(8,128)(2,1)}) %reduce-scatter.19.cloned.1.call-update) | async-done | bytes 262160
  436.1 7.5 fusion.35
  445.2 9.1 fusion.47
  454.3 9.4 fusion.45
  465.7 5.4 fusion.48
  472.5 40.3 %all-reduce.17 = (f32[1024]{0:T(1024)S(1)}, f32[1024]{0:T(1024)S(1)}, f32[1024]{0:T(1024)S(1)}, f32[1024]{0:T(1024)S(1)}, f32[1024]{0:T(1024)S(1)}, /*index=5*/f...) all-reduce(f32[1024]{0:T(1024)S(1)} %dynamic-update-slice.7, ...), channel_id=1, replica_groups=mesh['seq'=8,'fsdp'=4] {'seq','fsdp'}, use_global_device_ids=true, to_apply=%add.7 | all-reduce | flops 13312 | bytes 106496
  518.1 5.7 fusion.18
  523.8 62.1 %reduce-scatter.13.cloned.1.call-done = f32[32,1024]{1,0:T(8,128)} async-done(((f32[1024,1024]{1,0:T(8,128)}), f32[32,1024]{1,0:T(8,128)}) %reduce-scatter.13.cloned.1.call-update) | async-done | bytes 131088 | tf_op jit(solution)/shard_map/reduce_scatter | solution.py:198
  585.9 159.8 %reduce-scatter.11.cloned.1.call-done = f32[32,3072]{1,0:T(8,128)} async-done(((f32[1024,3072]{1,0:T(8,128)}), f32[32,3072]{1,0:T(8,128)}) %reduce-scatter.11.cloned.1.call-update) | async-done | bytes 393232 | tf_op jit(solution)/shard_map/reduce_scatter | solution.py:247
  745.7 362.5 %reduce-scatter.17.cloned.1.call-done = f32[128,1024]{1,0:T(8,128)} async-done(((f32[4096,1024]{1,0:T(8,128)}), f32[128,1024]{1,0:T(8,128)}) %reduce-scatter.17.cloned.1.call-update) | async-done | bytes 524304 | tf_op jit(solution)/shard_map/reduce_scatter | solution.py:184
  1108.2 364.7 %reduce-scatter.15.cloned.1.call-done = f32[32,4096]{1,0:T(8,128)} async-done(((f32[1024,4096]{1,0:T(8,128)}), f32[32,4096]{1,0:T(8,128)}) %reduce-scatter.15.cloned.1.call-update) | async-done | bytes 524304 | tf_op jit(solution)/shard_map/reduce_scatter | solution.py:190
  (163 shorter events, 73.4 us)
Async XLA Ops:
  7.2 76.5 %all-gather.9.cloned.1.call-start = ((), (), s32[]{:S(2)}) async-start(), calls=%async_computation.6 | async-start | bytes 6488064 | tf_op jit(solution)/shard_map/all_gather | solution.py:48
  8.9 114.9 %all-gather.11.cloned.1.call-start = ((), (), s32[]{:S(2)}) async-start(), calls=%async_computation.7 | async-start | bytes 1310720 | tf_op jit(solution)/shard_map/all_gather | solution.py:88
  88.5 23.9 %copy-start.24 = (s32[128]{0:T(128)S(1)}, s32[128]{0:T(128)}, u32[]{:S(2)}) copy-start(s32[128]{0:T(128)} %param.32) | copy-start | bytes 1540
  88.5 56.3 %all-gather.13.cloned.1.call-start = ((), (), s32[]{:S(2)}) async-start(), calls=%async_computation.8 | async-start | bytes 1310720 | tf_op jit(solution)/shard_map/all_gather | solution.py:87
  89.3 114.6 %all-gather.15.cloned.1.call-start = ((), (), s32[]{:S(2)}) async-start(), calls=%async_computation.9 | async-start | bytes 2162688 | tf_op jit(solution)/shard_map/all_gather | solution.py:49
  90.0 193.2 %all-gather.17.cloned.1.call-start = ((), (), s32[]{:S(2)}) async-start(), calls=%async_computation.10 | async-start | bytes 8650752 | tf_op jit(solution)/shard_map/all_gather | solution.py:52
  90.9 271.4 %all-gather.19.cloned.1.call-start = ((), (), s32[]{:S(2)}) async-start(), calls=%async_computation.11 | async-start | bytes 8650752 | tf_op jit(solution)/shard_map/all_gather | solution.py:53
  91.7 315.1 %reduce-scatter.21.cloned.1.call-start = ((), (), s32[]{:S(2)}) async-start(), calls=%async_computation.17 | async-start | bytes 1310720
  91.7 3.6 collective-permute-start
  95.4 4.5 collective-permute-start.1
  99.9 1.2 collective-permute-start.2
  101.1 18.9 %collective-permute-start.3 = (f32[1024]{0:T(1024)S(1)}, f32[1024]{0:T(1024)S(1)}, u32[]{:S(2)}, u32[]{:S(2)}) collective-permute-start(f32[1024]{0:T(1024)S(1)} %maximum_select_fusion.2), channel_id=1, source_target_pairs={{0,8},{1,9},{2,10},{3,11},{4,12},{5,13},{6,14},{7,15},{8,0},{9,1},... | collective-permute-start | bytes 12296 | tf_op jit(solution)/shard_map/ppermute | solution.py:16
  120.0 3.7 collective-permute-start.4
  125.6 22.9 %copy-start.9 = (bf16[512,1024]{0,1:T(8,128)(2,1)}, bf16[512,1024]{0,1:T(8,128)(2,1)S(1)}, u32[]{:S(2)}) copy-start(bf16[512,1024]{0,1:T(8,128)(2,1)S(1)} %copy.44) | copy-start | bytes 3145732
  149.2 54.7 %copy-start.3 = (bf16[128,1024]{1,0:T(8,128)(2,1)S(1)}, bf16[128,1024]{1,0:T(8,128)(2,1)}, u32[]{:S(2)}) copy-start(bf16[128,1024]{1,0:T(8,128)(2,1)} %param.17) | copy-start | bytes 786436
  150.7 132.5 %copy-start.19 = (bf16[16,64,128]{2,1,0:T(8,128)(2,1)}, bf16[16,64,128]{2,1,0:T(8,128)(2,1)S(1)}, u32[]{:S(2)}) copy-start(bf16[16,64,128]{2,1,0:T(8,128)(2,1)S(1)} %fusion.20) | copy-start | bytes 786436
  283.2 79.1 %copy-start.11 = (bf16[128,1024]{1,0:T(8,128)(2,1)S(1)}, bf16[128,1024]{1,0:T(8,128)(2,1)}, u32[]{:S(2)}) copy-start(bf16[128,1024]{1,0:T(8,128)(2,1)} %param.31) | copy-start | bytes 786436
  288.0 81.6 %copy-start.4 = (f32[128,4096]{1,0:T(8,128)}, f32[128,4096]{1,0:T(8,128)S(1)}, u32[]{:S(2)}) copy-start(f32[128,4096]{1,0:T(8,128)S(1)} %fusion.46) | copy-start | bytes 6291460
  380.8 54.2 %reduce-scatter.19.cloned.1.call-start = ((), (), s32[]{:S(2)}) async-start(), calls=%async_computation.16 | async-start | bytes 1310720
  389.5 196.5 %reduce-scatter.13.cloned.1.call-start = ((), (), s32[]{:S(2)}) async-start(), calls=%async_computation.13 | async-start | bytes 4325376 | tf_op jit(solution)/shard_map/reduce_scatter | solution.py:198
  393.4 352.4 %reduce-scatter.11.cloned.1.call-start = ((), (), s32[]{:S(2)}) async-start(), calls=%async_computation.12 | async-start | bytes 12976128 | tf_op jit(solution)/shard_map/reduce_scatter | solution.py:247
  408.0 35.6 %copy-start.13 = (bf16[128,1024]{0,1:T(8,128)(2,1)}, bf16[128,1024]{0,1:T(8,128)(2,1)S(1)}, u32[]{:S(2)}) copy-start(bf16[128,1024]{0,1:T(8,128)(2,1)S(1)} %copy.51) | copy-start | bytes 786436
  443.6 664.6 %reduce-scatter.17.cloned.1.call-start = ((), (), s32[]{:S(2)}) async-start(), calls=%async_computation.15 | async-start | bytes 17301504 | tf_op jit(solution)/shard_map/reduce_scatter | solution.py:184
  454.2 1018.6 %reduce-scatter.15.cloned.1.call-start = ((), (), s32[]{:S(2)}) async-start(), calls=%async_computation.14 | async-start | bytes 17301504 | tf_op jit(solution)/shard_map/reduce_scatter | solution.py:190
  (20 other events, 87.2 us)
Sparse Core Ops, SparseCore 0:
  11.4 72.1 all-gather.8
  88.6 26.5 all-gather.10
  117.4 27.3 all-gather.12
  148.1 55.7 all-gather.14
  207.3 75.9 all-gather.16
  286.6 75.6 all-gather.18
  380.9 25.9 reduce-scatter.20
  409.1 25.7 reduce-scatter.18
  437.8 148.1 reduce-scatter.12
  592.4 153.3 reduce-scatter.10
  748.6 359.5 reduce-scatter.16
  1110.9 361.9 reduce-scatter.14
